TPU v7x, 256 devices: a whole 4x4x8 slice. The times are simulated.
256 devices in a mesh: section: 16 (over y, z_lo), dp: 8 (over z_hi, x), tensor: 2 (over core).
Axes of the slice: x: 4, y: 4, z: 8 (z_hi: 2, z_lo: 4; z = z_hi * 4 + z_lo), core: 2. Of those that a mesh axis runs over, the one named last changes fastest.
Arguments:
- context: bfloat16 [16, 16, 256, 2048], P('section', 'dp'), may hold values from -6 to 6
- queries: bfloat16 [16, 16, 64, 2048], P('section', 'dp'), may hold values from -6 to 6
- lengths: int32 [16, 16], P('section', 'dp'), may hold values from 32 to 256
- norm_gain: float32 [16, 2048], P('section'), may hold values from 0.1 to 1.9
- qkv_weight: bfloat16 [16, 2048, 3, 2048], P('section', 'dp', None, 'tensor')
- out_weight: bfloat16 [16, 2048, 2048], P('section', 'tensor', 'dp'), may hold values from -0.5 to 0.5
Outputs:
- next_context: bfloat16 [16, 16, 256, 2048], P('section', 'dp')
- next_queries: bfloat16 [16, 16, 64, 2048], P('section', 'dp')
All inputs are finite; a program needn't handle non-finite values.
Results may differ from a plain program's by a relative error of at most 0.014.
The roundings to bfloat16 on the way count: a program that leaves them out, or rounds other values in their place, can miss the bound.
Values may be sent and summed in bfloat16 or wider, within the bound.
No kernel may reach another device: no remote copies, remote signals or barrier semaphores. Data moves between devices by JAX's collectives and lax.ppermute only.
A program may use at most 128 MiB of HBM per device.

v0:
```python
import math
import jax
import jax.numpy as jnp
from jax import lax
from jax.sharding import PartitionSpec as P

HEAD = 128


def from_behind(array, axis, by):
    count = lax.axis_size(axis)
    return lax.ppermute(array, axis, [(i, (i + by) % count) for i in range(count)])


def attend(projected, valid_len, first_row, row_count, memory_rows):
    query_part = projected[:, first_row : first_row + row_count, 0]
    key_part = projected[:, :memory_rows, 1]
    value_part = projected[:, :memory_rows, 2]
    scores = jnp.einsum(
        "brhd,bjhd->bhrj", query_part, key_part, preferred_element_type=jnp.float32
    ) * (1.0 / math.sqrt(HEAD))
    key_index = jnp.arange(memory_rows, dtype=jnp.int32)
    valid = key_index[None, None, None, :] < valid_len[:, None, None, None]
    scores = jnp.where(valid, scores, -1e30)
    top_score = jnp.max(scores, axis=-1, keepdims=True)
    expo = jnp.exp(scores - top_score)
    probs = (expo / jnp.sum(expo, axis=-1, keepdims=True)).astype(jnp.bfloat16)
    mixed = jnp.einsum(
        "bhrj,bjhd->brhd", probs, value_part, preferred_element_type=jnp.float32
    ).astype(jnp.bfloat16)
    return mixed


def per_device(context, queries, lengths, norm_gain, qkv_weight, out_weight):
    context_rows = context[0]
    query_rows = queries[0]
    stream_rows = jnp.concatenate([context_rows, query_rows], axis=1)
    scene_count = stream_rows.shape[0]
    row_total = stream_rows.shape[1]
    model_width = stream_rows.shape[2]
    memory_rows = context.shape[2]
    local_width = qkv_weight.shape[3]
    head_count = local_width // HEAD
    encoder_flag = lax.axis_index("section") < lax.axis_size("section") // 2
    widened = stream_rows.astype(jnp.float32)
    mean_square = jnp.mean(widened * widened, axis=-1, keepdims=True)
    normed = (widened * lax.rsqrt(mean_square + 1e-06) * norm_gain[0]).astype(jnp.bfloat16)
    flat_rows = normed.reshape(scene_count * row_total, model_width)
    weight_rows = lax.all_gather(qkv_weight, "dp", axis=1, tiled=True)
    row_count = weight_rows.shape[1]
    projected = jnp.dot(
        flat_rows,
        weight_rows[0].reshape(row_count, 3 * local_width),
        preferred_element_type=jnp.float32,
    )
    projected = projected.astype(jnp.bfloat16).reshape(scene_count, row_total, 3, head_count, HEAD)
    mixed = attend(projected, lengths[0], 0, row_total, memory_rows)
    row_index = jnp.arange(row_total, dtype=jnp.int32)
    keep_rows = jnp.where(encoder_flag, row_index < memory_rows, row_index >= memory_rows)
    mixed = mixed * keep_rows[None, :, None, None].astype(jnp.bfloat16)
    mixed_flat = mixed.reshape(scene_count * row_total, local_width)
    update = jnp.dot(
        mixed_flat,
        lax.all_gather(out_weight, "dp", axis=2, tiled=True)[0],
        preferred_element_type=jnp.float32,
    )
    update = update.reshape(scene_count, row_total, model_width)
    head_total = lax.psum(update.astype(jnp.bfloat16), "tensor").astype(jnp.float32)
    fresh = (widened + head_total).astype(jnp.bfloat16)
    context_new = fresh[:, :memory_rows]
    query_new = fresh[:, memory_rows:]
    passed = from_behind((context_new, query_new), "section", 1)
    return (passed[0][None], passed[1][None])


def solution(mesh):
    return jax.shard_map(
        per_device,
        mesh=mesh,
        in_specs=(
            P("section", "dp", None, None),
            P("section", "dp", None, None),
            P("section", "dp"),
            P("section", None),
            P("section", "dp", None, "tensor"),
            P("section", "tensor", "dp"),
        ),
        out_specs=(P("section", "dp", None, None), P("section", "dp", None, None)),
        check_vma=False,
    )
```

profile of v0, /device:TPU:1, one launch (start us, length us, event | category | flops | bytes accessed | tf_op | source)
XLA Modules:
  0.0 489.0 jit_solution(638077608019087004)
XLA Ops:
  7.3 2.7 copy.11
  10.0 0.0 all-gather.5.cloned.1.call-start
  10.1 0.7 all-gather.5.cloned.1.call-update
  10.8 0.6 fusion.1
  11.4 0.1 iota_compare_fusion.2
  11.5 2.2 fusion.3
  13.7 254.5 %all-gather.3.cloned.1.call-done = bf16[1,2048,3,1024]{1,3,2,0:T(8,128)(2,1)} async-done(((bf16[1,256,3,1024]{1,3,2,0:T(8,128)(2,1)}), bf16[1,2048,3,1024]{1,3,2,0:T(8,128)(2,1)}) %all-gather.3.cloned.1.call-update) | async-done | bytes 12582928 | tf_op jit(solution)/shard_map/all_gather | solution.py:49
  268.2 12.1 %fusion.15 = bf16[80,8,24,128]{3,1,2,0:T(8,128)(2,1)S(1)} fusion(bf16[640,2048]{1,0:T(8,128)(2,1)} %bitcast.43, bf16[2048,3072]{0,1:T(8,128)(2,1)} %bitcast.47), kind=kOutput, calls=%fused_computation.21 | convolution fusion | flops 8055029760 | bytes 19136512 | tf_op jit(solution)/shard_map/dot_general | solution.py:51
  280.3 1.1 copy.20
  281.5 0.1 slice.20
  281.5 0.4 fusion.24
  281.9 0.9 fusion.19
  282.8 2.4 fusion.25
  285.2 2.0 multiply_bitcast_fusion
  287.2 90.6 %all-gather.5.cloned.1.call-done = bf16[1,1024,2048]{2,1,0:T(8,128)(2,1)} async-done(((bf16[1,1024,256]{2,1,0:T(8,128)(2,1)}), bf16[1,1024,2048]{2,1,0:T(8,128)(2,1)}) %all-gather.5.cloned.1.call-update) | async-done | bytes 4194320 | tf_op jit(solution)/shard_map/all_gather | solution.py:64
  377.7 7.0 %fusion.8 = bf16[2,320,2048]{2,1,0:T(8,128)(2,1)} fusion(bf16[1,1024,2048]{2,1,0:T(8,128)(2,1)} %all-gather.5.cloned.1.call-done, bf16[2,8,40,8,128]{4,3,2,1,0:T(8,128)(2,1)} %multiply_bitcast_fusion), kind=kOutput, calls=%fused_computation.15 | convolution fusion | flops 2685665280 | bytes 8126464 | tf_op jit(solution)/shard_map/dot_general | solution.py:62
  384.7 30.4 %all-reduce.2.cloned.1.call-done = bf16[2,320,2048]{2,1,0:T(8,128)(2,1)} async-done(((bf16[2,320,2048]{2,1,0:T(8,128)(2,1)}), bf16[2,320,2048]{2,1,0:T(8,128)(2,1)}) %all-reduce.2.cloned.1.call-update) | async-done | bytes 2621456 | tf_op jit(solution)/shard_map/psum | solution.py:68
  415.2 2.8 fusion.4
  418.0 0.1 slice.23
  418.1 1.1 collective-permute-start
  419.3 1.4 collective-permute-start.1
  420.6 59.8 %collective-permute-done.1 = bf16[2,64,2048]{2,1,0:T(8,128)(2,1)S(1)} collective-permute-done((bf16[2,64,2048]{2,1,0:T(8,128)(2,1)S(1)}, bf16[2,64,2048]{2,1,0:T(8,128)(2,1)S(1)}, u32[]{:S(2)}, u32[]{:S(2)}) %collective-permute-start.1) | collective-permute-done | bytes 524320 | tf_op jit(solution)/shard_map/ppermute | solution.py:12
  480.4 1.3 copy.34
  481.7 0.8 copy.35
  (16 shorter events, 0.2 us)
Async XLA Ops:
  7.2 3.7 copy-start
  7.2 3.7 copy-start.1
  7.2 4.3 copy-start.3
  7.2 4.3 copy-start.2
  7.2 261.0 %all-gather.3.cloned.1.call-start = ((), (), s32[]{:S(2)}) async-start(), calls=%async_computation | async-start | bytes 14155776 | tf_op jit(solution)/shard_map/all_gather | solution.py:49
  10.0 367.7 %all-gather.5.cloned.1.call-start = ((), (), s32[]{:S(2)}) async-start(), calls=%async_computation.1 | async-start | bytes 4718592 | tf_op jit(solution)/shard_map/all_gather | solution.py:64
  10.8 404.4 %all-reduce.2.cloned.1.call-start = ((), (), s32[]{:S(2)}) async-start(), calls=%async_computation.2 | async-start | bytes 5242880 | tf_op jit(solution)/shard_map/psum | solution.py:68
  418.1 62.2 %collective-permute-start = (bf16[2,256,2048]{2,1,0:T(8,128)(2,1)S(1)}, bf16[2,256,2048]{2,1,0:T(8,128)(2,1)S(1)}, u32[]{:S(2)}, u32[]{:S(2)}) collective-permute-start(bf16[2,256,2048]{2,1,0:T(8,128)(2,1)S(1)} %slice.23), channel_id=1, source_target_pairs={{0,16},{16,32},{32,48},{48,64},{64,80},{80,96},{96,112},{112,128},... | collective-permute-start | bytes 6291464 | tf_op jit(solution)/shard_map/ppermute | solution.py:12
  419.3 61.1 %collective-permute-start.1 = (bf16[2,64,2048]{2,1,0:T(8,128)(2,1)S(1)}, bf16[2,64,2048]{2,1,0:T(8,128)(2,1)S(1)}, u32[]{:S(2)}, u32[]{:S(2)}) collective-permute-start(bf16[2,64,2048]{2,1,0:T(8,128)(2,1)S(1)} %slice.24), channel_id=1, source_target_pairs={{0,16},{16,32},{32,48},{48,64},{64,80},{80,96},{96,112},{112,128},... | collective-permute-start | bytes 1572872 | tf_op jit(solution)/shard_map/ppermute | solution.py:12
Sparse Core Ops, SparseCore 0:
  11.1 257.0 all-gather.2
  270.7 107.0 all-gather.4
  384.9 30.2 all-reduce.1
where the time goes:
time: 489 us
  waiting for transfers between devices  436 us (89%)
  matrix products  21.9 us (4%)
  between operations  13.9 us (3%)
  other arithmetic  8.03 us (2%)
  local copies, waits for them, and re-layouts  6.61 us (1%)
    all_gather x1, waiting for transfers between devices, per_device(): weight_rows = lax.all_gather(qkv_weight, 'dp', axis=1, tiled=True)  255 us
    all_gather x1, waiting for transfers between devices, per_device(): lax.all_gather(out_weight, 'dp', axis=2, tiled=True)[0]  90.6 us
    ppermute x2, waiting for transfers between devices, from_behind(): lax.ppermute(array, axis, [(i, (i + by) % count) for i in range(count)])  59.8 us
    psum x1, waiting for transfers between devices, per_device(): lax.psum(update.astype(jnp.bfloat16), 'tensor').astype(jnp.float32)  30.4 us
    dot_general x1, matrix products, per_device(): jnp.dot(flat_rows, weight_rows[0].reshape(row_count, 3 * local_width), pr...  12.1 us
  transfers between devices with their start and end apart: 5, of which 4 were waited for; matrix products, arithmetic and copies ran while one was open for 4% of the time, Pallas kernels for 0%

commit v1 on v0

--- a/solution.py
+++ b/solution.py
@@ -5,6 +5,12 @@
 from jax.sharding import PartitionSpec as P
 
 HEAD = 128
+
+
+def convert_heaps(sheet, comm_axis, k_dim=2):
+    r1 = jnp.stack(jax.lax.psum(1, axis_name=comm_axis) * [sheet])
+    before = jax.lax.all_to_all(r1, axis_name=comm_axis, split_axis=0, concat_axis=0)
+    return jnp.concatenate(before, k_dim)
 
 
 def from_behind(array, axis, by):
@@ -60,9 +66,7 @@
     mixed = mixed * keep_rows[None, :, None, None].astype(jnp.bfloat16)
     mixed_flat = mixed.reshape(scene_count * row_total, local_width)
     update = jnp.dot(
-        mixed_flat,
-        lax.all_gather(out_weight, "dp", axis=2, tiled=True)[0],
-        preferred_element_type=jnp.float32,
+        mixed_flat, convert_heaps(out_weight, "dp")[0], preferred_element_type=jnp.float32
     )
     update = update.reshape(scene_count, row_total, model_width)
     head_total = lax.psum(update.astype(jnp.bfloat16), "tensor").astype(jnp.float32)

time: 489 us -> 468 us (0.957)
  waiting for transfers between devices: 436 us -> 389 us
  local copies, waits for them, and re-layouts: 6.61 us -> 23.6 us
  starting transfers between devices: 2.56 us -> 14.3 us
    all_to_all x0 -> x1, waiting for transfers between devices: none -> 92.1 us  [convert_heaps(): jax.lax.all_to_all(r1, axis_name=comm_axis, split_axis=0, concat_axis=0)]
    all_gather x1 -> x0, waiting for transfers between devices: 90.6 us -> none  [per_device(): lax.all_gather(out_weight, 'dp', axis=2, tiled=True)[0]]
    all_gather x1, waiting for transfers between devices: 255 us -> 207 us  [per_device(): weight_rows = lax.all_gather(qkv_weight, 'dp', axis=1, tiled=True)]
    all_to_all x0 -> x1, starting transfers between devices: none -> 11.8 us  [convert_heaps(): jax.lax.all_to_all(r1, axis_name=comm_axis, split_axis=0, concat_axis=0)]
    another operation x0 -> x2, local copies, waits for them, and re-layouts: none -> 9.62 us  [the longest x1 7.41 us: per_device(): convert_heaps(out_weight, 'dp')[0]]
    reshape x0 -> x1, local copies, waits for them, and re-layouts: none -> 6.5 us  [convert_heaps(): return jnp.concatenate(before, k_dim)]
where the time goes in v1:
time: 468 us; the launch traced here: 467 us
  waiting for transfers between devices  389 us (83%)
  local copies, waits for them, and re-layouts  23.6 us (5%)
  matrix products  18.4 us (4%)
  starting transfers between devices  14.3 us (3%)
  between operations  14.2 us (3%)
  other arithmetic  8.04 us (2%)
    all_gather x1, waiting for transfers between devices, per_device(): weight_rows = lax.all_gather(qkv_weight, 'dp', axis=1, tiled=True)  207 us
    all_to_all x1, waiting for transfers between devices, convert_heaps(): jax.lax.all_to_all(r1, axis_name=comm_axis, split_axis=0, concat_axis=0)  92.1 us
    ppermute x2, waiting for transfers between devices, from_behind(): lax.ppermute(array, axis, [(i, (i + by) % count) for i in range(count)])  59.8 us
    psum x1, waiting for transfers between devices, per_device(): lax.psum(update.astype(jnp.bfloat16), 'tensor').astype(jnp.float32)  30.3 us
    dot_general x1, matrix products, per_device(): jnp.dot(flat_rows, weight_rows[0].reshape(row_count, 3 * local_width), pr...  12.1 us
    all_to_all x1, starting transfers between devices, convert_heaps(): jax.lax.all_to_all(r1, axis_name=comm_axis, split_axis=0, concat_axis=0)  11.8 us
  transfers between devices with their start and end apart: 5, of which 4 were waited for; matrix products, arithmetic and copies ran while one was open for 4% of the time, Pallas kernels for 0%

profile of v1, /device:TPU:1, one launch (start us, length us, event | category | flops | bytes accessed | tf_op | source)
XLA Modules:
  0.0 467.4 jit_solution(12416733342367653692)
XLA Ops:
  7.2 2.6 copy.16
  9.9 2.2 stack.2
  12.1 11.8 %all-to-all-start = ((bf16[8,1,1024,256]{3,2,1,0:T(8,128)(2,1)}), bf16[8,1,1024,256]{3,2,1,0:T(8,128)(2,1)}, u32[]{:S(2)}, u32[]{:S(2)}) async-start(bf16[8,1,1024,256]{3,2,1,0:T(8,128)(2,1)} %stack.2), calls=%async_computation | async-start | bytes 8388608 | tf_op jit(solution)/shard_map/all_to_all | solution.py:12
  23.9 0.6 fusion.1
  24.6 2.2 fusion.3
  26.8 92.1 %all-to-all-done = bf16[8,1,1024,256]{3,2,1,0:T(8,128)(2,1)} async-done(((bf16[8,1,1024,256]{3,2,1,0:T(8,128)(2,1)}), bf16[8,1,1024,256]{3,2,1,0:T(8,128)(2,1)}, u32[]{:S(2)}, u32[]{:S(2)}) %all-to-all-start) | async-done | bytes 4194336 | tf_op jit(solution)/shard_map/all_to_all | solution.py:12
  118.9 6.5 %copy.21 = bf16[1,1024,8,256]{3,2,1,0:T(8,128)(2,1)} copy(bf16[1,1024,8,256]{3,1,0,2:T(8,128)(2,1)} %bitcast.11) | data formatting | bytes 8388608 | tf_op jit(solution)/shard_map/reshape | solution.py:13
  125.4 7.4 %reshape.117 = bf16[1024,2048,1]{1,0,2:T(8,128)(2,1)} reshape(bf16[1,1024,8,256]{3,2,1,0:T(8,128)(2,1)} %copy.21) | data formatting | bytes 8388608 | tf_op jit(solution)/shard_map/squeeze;reshape | solution.py:69
  132.8 206.7 %all-gather.2.cloned.1.call-done = bf16[1,2048,3,1024]{1,3,2,0:T(8,128)(2,1)} async-done(((bf16[1,256,3,1024]{1,3,2,0:T(8,128)(2,1)}), bf16[1,2048,3,1024]{1,3,2,0:T(8,128)(2,1)}) %all-gather.2.cloned.1.call-update) | async-done | bytes 12582928 | tf_op jit(solution)/shard_map/all_gather | solution.py:55
  339.6 12.1 %fusion.10 = bf16[80,8,24,128]{3,1,2,0:T(8,128)(2,1)S(1)} fusion(bf16[640,2048]{1,0:T(8,128)(2,1)} %bitcast.42, bf16[2048,3072]{0,1:T(8,128)(2,1)} %bitcast.47), kind=kOutput, calls=%fused_computation.19 | convolution fusion | flops 8055029760 | bytes 19136512 | tf_op jit(solution)/shard_map/dot_general | solution.py:57
  351.7 1.1 copy.26
  352.8 0.4 fusion.19
  353.3 0.9 fusion.14
  354.2 2.4 fusion.20
  356.6 1.2 multiply_bitcast_fusion
  357.7 1.0 copy-done.2
  358.7 4.2 convolution_convert_fusion.1
  363.0 30.3 %all-reduce.2.cloned.1.call-done = bf16[2,320,2048]{2,1,0:T(8,128)(2,1)} async-done(((bf16[2,320,2048]{2,1,0:T(8,128)(2,1)}), bf16[2,320,2048]{2,1,0:T(8,128)(2,1)}) %all-reduce.2.cloned.1.call-update) | async-done | bytes 2621456 | tf_op jit(solution)/shard_map/psum | solution.py:72
  393.3 2.8 fusion.4
  396.2 1.1 collective-permute-start
  397.4 1.4 collective-permute-start.1
  398.7 59.8 %collective-permute-done.1 = bf16[2,64,2048]{2,1,0:T(8,128)(2,1)S(1)} collective-permute-done((bf16[2,64,2048]{2,1,0:T(8,128)(2,1)S(1)}, bf16[2,64,2048]{2,1,0:T(8,128)(2,1)S(1)}, u32[]{:S(2)}, u32[]{:S(2)}) %collective-permute-start.1) | collective-permute-done | bytes 524320 | tf_op jit(solution)/shard_map/ppermute | solution.py:18
  458.5 1.3 copy.40
  459.8 0.8 copy.41
  (22 shorter events, 0.5 us)
Async XLA Ops:
  7.2 2.7 copy-start.3
  7.2 332.4 %all-gather.2.cloned.1.call-start = ((), (), s32[]{:S(2)}) async-start(), calls=%async_computation.1 | async-start | bytes 14155776 | tf_op jit(solution)/shard_map/all_gather | solution.py:55
  12.1 11.8 %copy-start = (bf16[1,2,256,2048]{3,2,1,0:T(8,128)(2,1)S(1)}, bf16[1,2,256,2048]{3,2,1,0:T(8,128)(2,1)}, u32[]{:S(2)}) copy-start(bf16[1,2,256,2048]{3,2,1,0:T(8,128)(2,1)} %param.6) | copy-start | bytes 6291460
  12.1 11.8 %copy-start.1 = (bf16[1,2,64,2048]{3,2,1,0:T(8,128)(2,1)S(1)}, bf16[1,2,64,2048]{3,2,1,0:T(8,128)(2,1)}, u32[]{:S(2)}) copy-start(bf16[1,2,64,2048]{3,2,1,0:T(8,128)(2,1)} %param.7) | copy-start | bytes 1572868
  12.1 12.4 %copy-start.5 = (s32[1,2]{1,0:T(1,128)S(1)}, s32[1,2]{1,0:T(1,128)}, u32[]{:S(2)}) copy-start(s32[1,2]{1,0:T(1,128)} %param.8) | copy-start | bytes 28
  12.1 12.5 %copy-start.4 = (f32[1,2048]{1,0:T(1,128)S(1)}, f32[1,2048]{1,0:T(1,128)}, u32[]{:S(2)}) copy-start(f32[1,2048]{1,0:T(1,128)} %param.9) | copy-start | bytes 24580
  12.1 106.8 %all-to-all-start = ((bf16[8,1,1024,256]{3,2,1,0:T(8,128)(2,1)}), bf16[8,1,1024,256]{3,2,1,0:T(8,128)(2,1)}, u32[]{:S(2)}, u32[]{:S(2)}) async-start(bf16[8,1,1024,256]{3,2,1,0:T(8,128)(2,1)} %stack.2), calls=%async_computation | async-start | bytes 8388608 | tf_op jit(solution)/shard_map/all_to_all | solution.py:12
  23.8 369.4 %all-reduce.2.cloned.1.call-start = ((), (), s32[]{:S(2)}) async-start(), calls=%async_computation.2 | async-start | bytes 5242880 | tf_op jit(solution)/shard_map/psum | solution.py:72
  356.5 2.2 copy-start.2
  396.2 62.2 %collective-permute-start = (bf16[2,256,2048]{2,1,0:T(8,128)(2,1)S(1)}, bf16[2,256,2048]{2,1,0:T(8,128)(2,1)S(1)}, u32[]{:S(2)}, u32[]{:S(2)}) collective-permute-start(bf16[2,256,2048]{2,1,0:T(8,128)(2,1)S(1)} %slice.23), channel_id=1, source_target_pairs={{0,16},{16,32},{32,48},{48,64},{64,80},{80,96},{96,112},{112,128},... | collective-permute-start | bytes 6291464 | tf_op jit(solution)/shard_map/ppermute | solution.py:18
  397.4 61.1 %collective-permute-start.1 = (bf16[2,64,2048]{2,1,0:T(8,128)(2,1)S(1)}, bf16[2,64,2048]{2,1,0:T(8,128)(2,1)S(1)}, u32[]{:S(2)}, u32[]{:S(2)}) collective-permute-start(bf16[2,64,2048]{2,1,0:T(8,128)(2,1)S(1)} %slice.24), channel_id=1, source_target_pairs={{0,16},{16,32},{32,48},{48,64},{64,80},{80,96},{96,112},{112,128},... | collective-permute-start | bytes 1572872 | tf_op jit(solution)/shard_map/ppermute | solution.py:18
Sparse Core Ops, SparseCore 0:
  11.1 328.4 all-gather.1
  363.1 30.1 all-reduce.1
